TPU v7x, 32 devices: a whole 2x2x4 slice. The times are simulated.
32 devices in a mesh: grp: 2 (over y), row: 4 (over z), col: 4 (over x, core).
Axes of the slice: x: 2, y: 2, z: 4, core: 2. Of those that a mesh axis runs over, the one named last changes fastest.
Arguments:
- mask_param: float32 [2048, 1024], P(('grp', 'row'), 'col'), parts along dimension 0, may hold values from -6 to 6
- target: bfloat16 [2048, 1024], P(('grp', 'row'), 'col'), parts along dimension 0, may hold values from 0 to 1
- kernel_modes: float32 [12, 64, 128], replicated, may hold values from -24 to 24, as said below
- kernel_weight: float32 [12], replicated, may hold values from 0.02 to 0.2
Outputs:
- healed_param: float32 [2048, 1024], P(('grp', 'row'), 'col'), parts along dimension 0
There are 2 independent parts, one for each index of `grp`. A program takes and returns all parts, laid end to end along the dimension named above; an argument that names none is the same for every part. Nothing has to cross between parts.
Inputs may be any that keep to these rules, and one draw needn't show every extreme that they name: `kernel_modes`: the response of every kernel at the zero-frequency mode (row 32, columns 32 and 96) is zero.
All inputs are finite; a program needn't handle non-finite values.
Results may differ from a plain program's by a relative error of at most 0.0095.
Values may be sent and summed in bfloat16 or wider, within the bound.
No kernel may reach another device: no remote copies, remote signals or barrier semaphores. Data moves between devices by JAX's collectives and lax.ppermute only.
A program may use at most 64 MiB of HBM per device.

v0:
```python
import math

import jax
import jax.numpy as jnp
import numpy as np
from jax import lax
from jax.experimental import pallas as pl
from jax.experimental.pallas import tpu as pltpu
from jax.sharding import PartitionSpec as P


TILE = 256
MARGIN = 64
MODES = 64
KERN = 12
HALF = 128
WIN = 384
COARSE = 128
STEP = WIN // COARSE

threshold = 0.4
step_rate = 16.0
area = float(WIN * WIN)

VMEM = pltpu.VMEM
BF16 = jnp.bfloat16
F32 = jnp.float32


def tables():
    freq = np.arange(MODES) - MODES // 2
    angle = (2.0 * math.pi / WIN) * np.mod(freq[:, None] * np.arange(WIN)[None], WIN)
    cos, sin = np.cos(angle), np.sin(angle)
    stacked = np.concatenate([cos, sin], 0)
    forward = stacked.T
    core = slice(MARGIN, MARGIN + TILE)
    c_core, s_core = cos[:, core], sin[:, core]
    c_low, s_low = cos[:, ::STEP], sin[:, ::STEP]
    reach = HALF + MARGIN
    place_a = np.zeros((TILE, 2 * MODES))
    place_a[TILE - reach :] = forward[:reach]
    place_b = np.zeros((TILE, 2 * MODES))
    place_b[:reach] = forward[reach:]
    offset = np.arange(MARGIN, MARGIN + TILE)[:, None] - STEP * np.arange(COARSE)[None]
    orders = np.arange(1, 2 * MODES // 2)
    interp = 1.0 + 2.0 * np.cos((2.0 * math.pi / WIN) * orders[:, None, None] * offset[None]).sum(0)
    interp = (interp + np.cos((2.0 * math.pi / WIN) * MODES * offset)) / COARSE
    high = interp.astype(jnp.bfloat16).astype(np.float64)
    pad = np.zeros((COARSE, COARSE))
    table = dict(
        own=(forward[core], np.concatenate([c_core.T, -s_core.T], 1)),
        rim=(
            np.concatenate([forward[MARGIN + TILE :], forward[:MARGIN]], 0),
            np.concatenate([stacked[:, :MARGIN], stacked[:, MARGIN + TILE :]], 1),
        ),
        q_own=(stacked[:, core],),
        spread=(np.block([[c_low, s_low], [-s_low, c_low]]),),
        q_low=(np.concatenate([c_low.T, s_low.T], 1), pad),
        interp=(high, interp - high),
        interp_t=(np.concatenate([high.T, (interp - high).T], 0),),
        gather=(
            np.block(
                [[c_low.T, -s_low.T, -s_low.T, -c_low.T], [s_low.T, c_low.T, c_low.T, -s_low.T]]
            ),
        ),
        q_back=(c_low, s_low),
        inv_left=(np.block([[c_core[:, HALF:], s_core[:, HALF:]], [-s_core[:, HALF:], c_core[:, HALF:]]]),),
        inv_right=(np.block([[c_core[:, :HALF], s_core[:, :HALF]], [-s_core[:, :HALF], c_core[:, :HALF]]]),),
        place=(place_a, place_b),
        q_place=(np.concatenate([place_a.T, place_b.T], 0),),
    )
    table = {name: np.concatenate(value, 1) for name, value in table.items()}
    arrays, rows = [], {}
    for names in (("own", "rim"), tuple(name for name in table if name not in ("own", "rim"))):
        start = 0
        for name in names:
            rows[name] = slice(start, start + len(table[name]))
            start = rows[name].stop
        arrays.append(np.concatenate([table[name] for name in names], 0).astype(jnp.bfloat16))
    place = table["place"].astype(jnp.bfloat16).astype(np.float64)
    sums = 0.5 * place.sum(0)
    level = []
    for q in (place[:, : 2 * MODES].sum(0), place[:, 2 * MODES :].sum(0)):
        for t in (sums[: 2 * MODES], sums[2 * MODES :]):
            c, s = slice(0, MODES), slice(MODES, 2 * MODES)
            real = np.outer(q[c], t[c]) - np.outer(q[s], t[s])
            imag = -np.outer(q[c], t[s]) - np.outer(q[s], t[c])
            level.append(np.concatenate([real, imag], 1) / area)
    level.append(np.concatenate([sums.reshape(2, 2 * MODES), np.zeros((6, 2 * MODES))], 0))
    return arrays + [np.concatenate(level, 0).astype(np.float32)], rows


(EDGE_TABLE, MAIN_TABLE, LEVEL_TABLE), TABLE_ROWS = tables()


class Tables:
    def __init__(self, ref):
        self.ref = ref

    def __getitem__(self, name):
        return self.ref[TABLE_ROWS[name], :]

    def left(self, name):
        return self.ref[TABLE_ROWS[name], :COARSE]

    def right(self, name):
        return self.ref[TABLE_ROWS[name], COARSE:]


def dot(left, right):
    return jnp.dot(left, right, preferred_element_type=F32)


def swap_halves(value):
    return pltpu.roll(value, MODES, axis=1)


def low_lanes(shape):
    return lax.broadcasted_iota(jnp.int32, shape, 1) < MODES


def modes_of(blocks):
    top, bottom = blocks[:MODES], swap_halves(blocks[MODES:])
    return jnp.where(low_lanes(top.shape), top - bottom, -(top + bottom)) / area


def imaging_modes(windows, resp_ref, swapped_ref, scaled_ref, cross_ref, weight_ref, field_ref, t):
    count = len(windows)
    low = low_lanes((MODES, 2 * MODES))
    cuts = 2 if count == 1 else 1
    groups = [range(i * KERN // cuts, (i + 1) * KERN // cuts) for i in range(cuts)]
    partials = []
    for spec, _, _ in windows:
        swapped = swap_halves(spec)
        spec_a = jnp.where(low, spec, swapped)
        spec_b = jnp.where(low, -swapped, spec)
        partial = []
        for group in groups:
            filtered = [(resp_ref[k] * spec_a + swapped_ref[k] * spec_b).astype(BF16) for k in group]
            spread = dot(jnp.concatenate(filtered, 0), t["spread"]).astype(BF16)
            partial += [spread[i * MODES : (i + 1) * MODES] for i in range(len(group))]
        partials.append(partial)
    levels = []
    for w, partial in enumerate(partials):
        chains = [jnp.zeros((COARSE, COARSE), F32)] * 2
        for k, part in enumerate(partial):
            real, imag = part[:, :COARSE], part[:, COARSE:]
            rotated = jnp.concatenate([part, jnp.concatenate([-imag, real], 1)], 0)
            field = dot(t.left("q_low"), rotated)
            field_ref[w * KERN + k] = field
            a_real, a_imag = field[:, :COARSE], field[:, COARSE:]
            chains[k % 2] = chains[k % 2] + weight_ref[k : k + 1, :] * (
                a_real * a_real + a_imag * a_imag
            )
        level = chains[0] + chains[1]
        levels.append((2.0 * level - 2.0 * threshold).astype(BF16))
    halves = [dot(t["interp"], jnp.concatenate([level, level], 0)).astype(BF16) for level in levels]
    cores = [dot(jnp.concatenate([half, half], 1), t["interp_t"]) for half in halves]
    lows = []
    for core, (_, goal, inner) in zip(cores, windows):
        rise = jnp.tanh(core)
        core_grad = ((rise + (1.0 - 2.0 * goal.astype(F32))) * (1.0 - rise * rise)).astype(BF16)
        rows_low, cols_low = t["interp_t"][:COARSE], t.left("interp")
        inner_row, inner_col = inner
        if inner_row is not None:
            outer = jnp.where(inner_row, rows_low[:, HALF:].astype(F32), 0.0).astype(BF16)
            rows_low = jnp.concatenate([rows_low[:, :HALF], outer], 1)
        if inner_col is not None:
            outer = jnp.where(inner_col, cols_low[HALF:].astype(F32), 0.0).astype(BF16)
            cols_low = jnp.concatenate([cols_low[:HALF], outer], 0)
        lows.append((dot(rows_low, core_grad).astype(BF16), cols_low))
    lows = [dot(left, right) for left, right in lows]
    gathers = []
    for w, low_grad in enumerate(lows):
        both = jnp.concatenate([low_grad, low_grad], 1)
        gathered = []
        for group in groups:
            shaded = [(field_ref[w * KERN + k] * both).astype(BF16) for k in group]
            rows = dot(jnp.concatenate(shaded, 0), t["gather"]).astype(BF16)
            gathered += [rows[i * COARSE : (i + 1) * COARSE] for i in range(len(group))]
        gathers.append(gathered)
    results = []
    for gathered in gathers:
        direct = jnp.zeros((MODES, 2 * MODES), F32)
        crossed = jnp.zeros((MODES, 2 * MODES), F32)
        for k in range(0, KERN, 2):
            one, two = gathered[k], gathered[k + 1]
            upper = jnp.concatenate([one[:, :COARSE], two[:, :COARSE]], 1)
            lower = jnp.concatenate([one[:, COARSE:], two[:, COARSE:]], 1)
            back = dot(t["q_back"], jnp.concatenate([upper, lower], 0))
            for i, part in enumerate((back[:, : 2 * MODES], back[:, 2 * MODES :])):
                direct = direct + scaled_ref[k + i] * part
                crossed = crossed + cross_ref[k + i] * part
        results.append(
            jnp.where(low, direct + swap_halves(direct), crossed - swap_halves(crossed)).astype(BF16)
        )
    return results


def edges_kernel(mask_ref, left_ref, right_ref, mask_out_ref):
    low = low_lanes((TILE, 2 * MARGIN))
    edge = jax.nn.sigmoid(jnp.where(low, mask_ref[:, : 2 * MARGIN], mask_ref[:, HALF:]))
    top, bottom = edge[:HALF], edge[HALF:]
    low = low[:HALF]
    left_ref[...] = jnp.where(low, top, swap_halves(bottom)).astype(BF16)
    right_ref[...] = jnp.where(low, swap_halves(top), bottom).astype(BF16)
    mask_out_ref[...] = mask_ref[...]


def goals_kernel(target_ref, after_ref, left_ref, right_ref, target_out_ref):
    left_ref[...] = target_ref[:, :HALF]
    right_ref[...] = target_ref[:, HALF:]
    target_out_ref[...] = target_ref[...]


def table_kernel(table_ref, kernel_weight_ref, after_ref, out_ref, weight_ref):
    out_ref[...] = table_ref[...]
    weights = kernel_weight_ref[...]
    for k in range(KERN):
        weight_ref[k : k + 1, :] = jnp.broadcast_to(weights[:, k : k + 1], (1, COARSE))


def by_parity(odd, even_ref, odd_ref, below, above):
    @pl.when(odd)
    def _():
        even_ref[...] = above
        odd_ref[...] = below

    @pl.when(jnp.logical_not(odd))
    def _():
        even_ref[...] = below
        odd_ref[...] = above


def below_above(odd, even_ref, odd_ref):
    even, odd_value = even_ref[...].astype(F32), odd_ref[...].astype(F32)
    return jnp.where(odd, odd_value, even), jnp.where(odd, even, odd_value)


def strip_kernel(cols, mask_ref, left_ref, right_ref, table_ref, u_ref, even_ref, odd_ref):
    t = Tables(table_ref)
    col = lax.axis_index("col")
    odd = lax.rem(lax.axis_index("row"), 2) == 1
    wire = jax.nn.sigmoid(mask_ref[...]).astype(BF16)
    low = low_lanes((HALF, 2 * MARGIN))
    right = jnp.where(col < cols - 1, right_ref[...].astype(F32), 0.0)
    left = jnp.where(col > 0, left_ref[...].astype(F32), 0.0)
    rim = jnp.concatenate(
        [jnp.where(low, right, swap_halves(left)), jnp.where(low, swap_halves(right), left)], 0
    ).astype(BF16)
    half_spec = (dot(wire, t.left("own")) + dot(rim, t.left("rim"))).astype(BF16)
    u_ref[...] = half_spec
    by_parity(odd, even_ref, odd_ref, half_spec[TILE - MARGIN :], half_spec[:MARGIN])


def goal_rows_kernel(target_ref, left_ref, right_ref, after_ref, even_ref, odd_ref):
    odd = lax.rem(lax.axis_index("row"), 2) == 1
    goals = jnp.concatenate([left_ref[...], target_ref[...], right_ref[...]], 1)
    by_parity(odd, even_ref, odd_ref, goals[HALF:], goals[:HALF])


def first_kernel(
    rows, mask_ref, u_ref, even_ref, odd_ref, goal_ref, resp_ref, weight_ref,
    edge_table_ref, table_ref, level_ref, first_ref, left_ref, right_ref, swapped_ref, scaled_ref, cross_ref,
    field_ref,
):
    for k in range(KERN):
        weight = weight_ref[k : k + 1, :]
        swapped = swap_halves(resp_ref[k])
        swapped_ref[k] = swapped
        scaled_ref[k] = (2.0 * weight) * resp_ref[k]
        cross_ref[k] = (2.0 * weight) * swapped
    edge, t = Tables(edge_table_ref), Tables(table_ref)
    row = lax.axis_index("row")
    below, above = below_above(lax.rem(row, 2) == 1, even_ref, odd_ref)
    above = jnp.where(row > 0, above, 0.0)
    below = jnp.where(row < rows - 1, below, 0.0)
    rim = jnp.concatenate([above, below], 0).astype(BF16)
    spec = modes_of(dot(t["q_own"], u_ref[...]) + dot(edge.right("rim"), rim))
    (combined,) = imaging_modes(
        [(spec, goal_ref[...], (None, None))], resp_ref, swapped_ref, scaled_ref, cross_ref,
        weight_ref, field_ref, t,
    )
    left = dot(combined, t["inv_right"]).astype(BF16)
    right = dot(combined, t["inv_left"]).astype(BF16)
    real = jnp.concatenate([left[:, :HALF], right[:, :HALF]], 1)
    imag = jnp.concatenate([left[:, HALF:], right[:, HALF:]], 1)
    mask_grad = dot(edge.right("own"), jnp.concatenate([real, imag], 0))
    mask = mask_ref[...]
    first = updated(mask, mask_grad)
    first_ref[...] = first
    sums = jnp.concatenate([level_ref[4 * MODES : 4 * MODES + 1, :], level_ref[4 * MODES + 1 : 4 * MODES + 2, :]], 1)
    half = dot(jax.nn.sigmoid(first).astype(BF16), t["place"]) - sums
    blocks = dot(t["q_place"], half.astype(BF16))
    right_ref[:MODES, :] = modes_of(blocks[:HALF, :HALF]).astype(BF16)
    left_ref[:MODES, :] = modes_of(blocks[:HALF, HALF:]).astype(BF16)
    right_ref[MODES:, :] = modes_of(blocks[HALF:, :HALF]).astype(BF16)
    left_ref[MODES:, :] = modes_of(blocks[HALF:, HALF:]).astype(BF16)


def updated(param, grad):
    rise = jnp.tanh(0.5 * param)
    return param - (step_rate / 4.0 / area) * (grad * (1.0 - rise * rise))


def columns_kernel(cols, own_left_ref, own_right_ref, left_ref, right_ref, even_ref, odd_ref):
    col = lax.axis_index("col")
    odd = lax.rem(lax.axis_index("row"), 2) == 1
    own = own_right_ref[...].astype(F32) + jnp.where(col < cols - 1, right_ref[...].astype(F32), 0.0)
    before = own_left_ref[...].astype(F32) + jnp.where(col > 0, left_ref[...].astype(F32), 0.0)
    below = jnp.concatenate([own[:MODES], before[:MODES]], 0).astype(BF16)
    above = jnp.concatenate([own[MODES:], before[MODES:]], 0).astype(BF16)
    by_parity(odd, even_ref, odd_ref, below, above)


def heal_kernel(
    rows, cols, first_ref, even_own_ref, odd_own_ref, even_ref, odd_ref, goal_ref, left_ref,
    right_ref, even_goal_ref, odd_goal_ref, resp_ref, swapped_ref, scaled_ref, cross_ref,
    weight_ref, edge_table_ref, table_ref, level_ref, out_ref, field_ref,
):
    edge, t = Tables(edge_table_ref), Tables(table_ref)
    row, col = lax.axis_index("row"), lax.axis_index("col")
    odd = lax.rem(row, 2) == 1
    inner_row, inner_col = row < rows - 1, col < cols - 1
    lower, upper = below_above(odd, even_own_ref, odd_own_ref)
    below, above = below_above(odd, even_ref, odd_ref)
    lower = lower + jnp.where(inner_row, below, 0.0)
    upper = upper + jnp.where(row > 0, above, 0.0)
    aa, ab, ba, bb = (level_ref[i * MODES : (i + 1) * MODES, :] for i in range(4))
    own_columns = aa + jnp.where(inner_col, ab, 0.0), ba + jnp.where(inner_col, bb, 0.0)
    both_columns = aa + ab, ba + bb
    lower = lower + jnp.concatenate(
        [a + jnp.where(inner_row, b, 0.0) for a, b in (own_columns, both_columns)], 0
    )
    upper = upper + jnp.concatenate([a + b for a, b in (own_columns, both_columns)], 0)
    own_goals = jnp.concatenate([left_ref[...], goal_ref[...], right_ref[...]], 1)
    goals_below, goals_above = below_above(odd, even_goal_ref, odd_goal_ref)
    goals_lower = jnp.concatenate([own_goals[HALF:].astype(F32), goals_below], 0)
    goals_upper = jnp.concatenate([goals_above, own_goals[:HALF].astype(F32)], 0)
    lower_right, lower_left, upper_right, upper_left = imaging_modes(
        [
            (lower[:MODES], goals_lower[:, TILE:], (inner_row, inner_col)),
            (lower[MODES:], goals_lower[:, :TILE], (inner_row, None)),
            (upper[:MODES], goals_upper[:, TILE:], (None, inner_col)),
            (upper[MODES:], goals_upper[:, :TILE], (None, None)),
        ],
        resp_ref, swapped_ref, scaled_ref, cross_ref, weight_ref, field_ref, t,
    )

    def kept(value, flag):
        return jnp.where(flag, value.astype(F32), 0.0).astype(BF16)

    left = jnp.concatenate(
        [kept(lower_left, col > 0), kept(upper_left, jnp.logical_and(row > 0, col > 0))], 0
    )
    right = jnp.concatenate([lower_right, kept(upper_right, row > 0)], 0)
    left = dot(left, t["inv_left"]).astype(BF16)
    right = dot(right, t["inv_right"]).astype(BF16)

    def quarter(modes):
        real = jnp.concatenate([left[modes, :HALF], right[modes, :HALF]], 1)
        imag = jnp.concatenate([left[modes, HALF:], right[modes, HALF:]], 1)
        return jnp.concatenate([real, imag], 0)

    q_inv = edge.right("own")
    below = dot(q_inv[:HALF], quarter(slice(0, MODES)))
    above = dot(q_inv[HALF:], quarter(slice(MODES, 2 * MODES)))
    out_ref[:HALF, :] = updated(first_ref[:HALF, :], above)
    out_ref[HALF:, :] = updated(first_ref[HALF:, :], below)


COST = {
    name: pl.CostEstimate(flops=int(micros * 1.1e9), bytes_accessed=1 << 16, transcendentals=0)
    for name, micros in (
        ("edges", 1.0), ("goals", 1.0), ("table", 1.0), ("strip", 1.0), ("goal_rows", 1.0),
        ("first", 3.0), ("columns", 1.0), ("heal", 5.0),
    )
}
VMEM_SPEC = pl.BlockSpec(memory_space=VMEM)
SMEM_SPEC = pl.BlockSpec(memory_space=pltpu.SMEM)


def fields(windows):
    return [VMEM((windows * KERN, COARSE, 2 * COARSE), F32)]


def shape_of(rows, cols, dtype):
    return jax.ShapeDtypeStruct((rows, cols), dtype)


def per_device(rows, cols, mask_param, target, kernel_modes, kernel_weight):
    table, edge_table = jnp.asarray(MAIN_TABLE), jnp.asarray(EDGE_TABLE)
    level = jnp.asarray(LEVEL_TABLE)

    def permuted(value, place):
        pairs = [
            (r * cols + c, place(r, c)[0] * cols + place(r, c)[1])
            for r in range(rows)
            for c in range(cols)
        ]
        return lax.ppermute(value, ("row", "col"), pairs)

    def move(value, down, right):
        return permuted(value, lambda r, c: ((r + down) % rows, (c + right) % cols))

    def swap(value, parity):
        def place(r, c):
            other = r + 1 if r % 2 == parity else r - 1
            return (other, c) if 0 <= other < rows else (r, c ^ 1)

        return permuted(value, place)

    def call(kernel, outs, other, limit, scratch, name, *args):
        return pl.pallas_call(
            kernel, out_shape=outs, in_specs=[other.get(i, VMEM_SPEC) for i in range(len(args))],
            out_specs=jax.tree.map(lambda _: VMEM_SPEC, outs), scratch_shapes=scratch,
            compiler_params=pltpu.CompilerParams(vmem_limit_bytes=limit),
            cost_estimate=COST[name],
        )(*args)

    edge_shape = shape_of(HALF, 2 * MARGIN, BF16)
    to_left, to_right, mask = call(
        edges_kernel, (edge_shape, edge_shape, shape_of(TILE, TILE, F32)), {}, 4 << 20, (),
        "edges", mask_param,
    )
    from_right = move(to_left, 0, -1)
    from_left = move(to_right, 0, 1)
    goal_shape = shape_of(TILE, HALF, BF16)
    goal_left, goal_right, goal = call(
        goals_kernel, (goal_shape, goal_shape, shape_of(TILE, TILE, BF16)), {}, 4 << 20, (),
        "goals", target, to_right,
    )
    goal_right, goal_left = move(goal_left, 0, -1), move(goal_right, 0, 1)
    edge_table, weights = call(
        table_kernel, (shape_of(*EDGE_TABLE.shape, BF16), shape_of(KERN, COARSE, F32)), {},
        4 << 20, (), "table", edge_table, kernel_weight.reshape(1, KERN), to_right,
    )
    rim_shape = shape_of(MARGIN, 2 * MODES, BF16)
    half_spec, even_rim, odd_rim = call(
        lambda *refs: strip_kernel(cols, *refs),
        (shape_of(TILE, 2 * MODES, BF16), rim_shape, rim_shape), {}, 4 << 20, (), "strip",
        mask, from_left, from_right, edge_table,
    )
    goal_shape = shape_of(HALF, 2 * TILE, BF16)
    even_goal, odd_goal = call(
        goal_rows_kernel, (goal_shape, goal_shape), {}, 4 << 20, (), "goal_rows",
        goal, goal_left, goal_right, even_rim,
    )
    odd_rim = swap(odd_rim, 1)
    even_rim = swap(even_rim, 0)
    even_goal = swap(even_goal, 0)
    odd_goal = swap(odd_goal, 1)
    pair_shape = shape_of(2 * MODES, 2 * MODES, BF16)
    resp_shape = jax.ShapeDtypeStruct(kernel_modes.shape, F32)
    first, to_left, to_right, *responses = call(
        lambda *refs: first_kernel(rows, *refs),
        (shape_of(TILE, TILE, F32), pair_shape, pair_shape)
        + (resp_shape,) * 3,
        {}, 16 << 20, fields(1), "first", mask, half_spec, even_rim, odd_rim, goal, kernel_modes,
        weights, edge_table, table, level,
    )
    from_right = move(to_left, 0, -1)
    from_left = move(to_right, 0, 1)
    even_own, odd_own = call(
        lambda *refs: columns_kernel(cols, *refs), (pair_shape, pair_shape), {}, 4 << 20, (),
        "columns", to_left, to_right, from_left, from_right,
    )
    even_modes = swap(even_own, 0)
    odd_modes = swap(odd_own, 1)
    return call(
        lambda *refs: heal_kernel(rows, cols, *refs), shape_of(TILE, TILE, F32),
        {}, 24 << 20, fields(4), "heal",
        first, even_own, odd_own, even_modes, odd_modes, goal, goal_left,
        goal_right, even_goal, odd_goal, kernel_modes, *responses, weights, edge_table,
        table, level,
    )


def solution(mesh):
    rows, cols = mesh.shape["row"], mesh.shape["col"]
    tile = P(("grp", "row"), "col")

    def body(*args):
        return per_device(rows, cols, *args)

    return jax.shard_map(
        body, mesh=mesh, in_specs=(tile, tile, P(), P()), out_specs=tile, check_vma=False
    )
```

profile of v0, /device:TPU:0, one launch (start us, length us, event | category | flops | bytes accessed | tf_op | source)
XLA Modules:
  0.0 26.4 jit_solution(12230530280359498361)
XLA Ops:
  0.0 0.0 copy-start.1
  0.0 0.9 %copy-done.1 = f32[256,256]{1,0:T(8,128)S(1)} copy-done((f32[256,256]{1,0:T(8,128)S(1)}, f32[256,256]{1,0:T(8,128)}, u32[]{:S(2)}) %copy-start.1) | copy-done | bytes 262168
  1.0 0.0 copy-start.5
  1.0 0.1 shard_map.73
  1.1 0.5 %collective-permute-start = (bf16[128,128]{1,0:T(8,128)(2,1)S(1)}, bf16[128,128]{1,0:T(8,128)(2,1)S(1)}, u32[]{:S(2)}, u32[]{:S(2)}) collective-permute-start(bf16[128,128]{1,0:T(8,128)(2,1)S(1)} %get-tuple-element.27.after_ref), channel_id=1, source_target_pairs={{0,1},{1,2},{2,3},{3,0},{4,5},{5,6},{6,7},{7,4},{8,9},{9,10},{10,1... | collective-permute-start | bytes 98312 | tf_op jit(solution)/shard_map/ppermute | solution.py:401
  1.6 0.0 copy-start.3
  1.6 2.0 %collective-permute-start.1 = (bf16[128,128]{1,0:T(8,128)(2,1)S(1)}, bf16[128,128]{1,0:T(8,128)(2,1)S(1)}, u32[]{:S(2)}, u32[]{:S(2)}) collective-permute-start(bf16[128,128]{1,0:T(8,128)(2,1)S(1)} %get-tuple-element.28), channel_id=1, source_target_pairs={{0,3},{1,0},{2,1},{3,2},{4,7},{5,4},{6,5},{7,6},{8,11},{9,8},{10,9... | collective-permute-start | bytes 98312 | tf_op jit(solution)/shard_map/ppermute | solution.py:401
  3.6 0.0 copy-done.5
  3.6 0.0 copy-done.3
  3.6 0.1 shard_map.74
  3.7 1.4 %collective-permute-done.refs_1_ = bf16[128,128]{1,0:T(8,128)(2,1)S(1)} collective-permute-done((bf16[128,128]{1,0:T(8,128)(2,1)S(1)}, bf16[128,128]{1,0:T(8,128)(2,1)S(1)}, u32[]{:S(2)}, u32[]{:S(2)}) %collective-permute-start) | collective-permute-done | bytes 32800 | tf_op jit(solution)/shard_map/ppermute | solution.py:401
  5.1 0.2 collective-permute-done.1.refs_2_
  5.3 0.0 copy-start.2
  5.3 0.2 shard_map.75
  5.5 2.3 %collective-permute-start.2 = (bf16[64,128]{1,0:T(8,128)(2,1)S(1)}, bf16[64,128]{1,0:T(8,128)(2,1)S(1)}, u32[]{:S(2)}, u32[]{:S(2)}) collective-permute-start(bf16[64,128]{1,0:T(8,128)(2,1)S(1)} %get-tuple-element.31.after_ref), channel_id=1, source_target_pairs={{0,4},{1,5},{2,6},{3,7},{4,0},{5,1},{6,2},{7,3},{8,12},{9,13},{10,... | collective-permute-start | bytes 49160 | tf_op jit(solution)/shard_map/ppermute | solution.py:401
  7.8 0.0 copy-start
  7.8 0.0 copy-start.4
  7.8 0.0 copy-start.6
  7.8 1.3 %collective-permute-start.3 = (bf16[64,128]{1,0:T(8,128)(2,1)S(1)}, bf16[64,128]{1,0:T(8,128)(2,1)S(1)}, u32[]{:S(2)}, u32[]{:S(2)}) collective-permute-start(bf16[64,128]{1,0:T(8,128)(2,1)S(1)} %get-tuple-element.32), channel_id=1, source_target_pairs={{0,1},{1,0},{2,3},{3,2},{4,8},{5,9},{6,10},{7,11},{8,4},{9,5},{10,... | collective-permute-start | bytes 49160 | tf_op jit(solution)/shard_map/ppermute | solution.py:401
  9.2 0.0 copy-done.2
  9.2 0.1 collective-permute-start.8
  9.3 1.7 %collective-permute-start.9 = (bf16[256,128]{1,0:T(8,128)(2,1)S(1)}, bf16[256,128]{1,0:T(8,128)(2,1)S(1)}, u32[]{:S(2)}, u32[]{:S(2)}) collective-permute-start(bf16[256,128]{1,0:T(8,128)(2,1)S(1)} %get-tuple-element.41), channel_id=1, source_target_pairs={{0,3},{1,0},{2,1},{3,2},{4,7},{5,4},{6,5},{7,6},{8,11},{9,8},{10,9... | collective-permute-start | bytes 196616 | tf_op jit(solution)/shard_map/ppermute | solution.py:401
  11.0 0.0 collective-permute-done.2.refs_2_
  11.0 0.0 collective-permute-done.3.refs_3_
  11.0 0.0 copy-done
  11.0 0.0 copy-done.4
  11.0 0.0 copy-done.6
  11.0 2.7 %shard_map.77 = (f32[256,256]{1,0:T(8,128)S(1)}, bf16[128,128]{1,0:T(8,128)(2,1)S(1)}, bf16[128,128]{1,0:T(8,128)(2,1)S(1)}, f32[12,64,128]{2,1,0:T(8,128)S(1)},...) custom-call(f32[256,256]{1,0:T(8,128)S(1)} %get-tuple-element.26.refs_0_, ...), custom_call_target="tpu_custom_call" | custom-call | flops 3300000000 | bytes 65536 | tf_op jit(solution)/shard_map/pallas_call | solution.py:414
  13.8 0.1 collective-permute-start.4
  13.8 1.7 %collective-permute-start.5 = (bf16[128,128]{1,0:T(8,128)(2,1)S(1)}, bf16[128,128]{1,0:T(8,128)(2,1)S(1)}, u32[]{:S(2)}, u32[]{:S(2)}) collective-permute-start(bf16[128,128]{1,0:T(8,128)(2,1)S(1)} %get-tuple-element.36.refs_0_), channel_id=1, source_target_pairs={{0,3},{1,0},{2,1},{3,2},{4,7},{5,4},{6,5},{7,6},{8,11},{9,8},{10,9... | collective-permute-start | bytes 98312 | tf_op jit(solution)/shard_map/ppermute | solution.py:401
  15.6 0.0 collective-permute-done.8.left_ref.refs_6_
  15.6 0.0 collective-permute-done.9.right_ref.refs_7_
  15.6 1.9 %collective-permute-start.10 = (bf16[128,512]{1,0:T(8,128)(2,1)S(1)}, bf16[128,512]{1,0:T(8,128)(2,1)S(1)}, u32[]{:S(2)}, u32[]{:S(2)}) collective-permute-start(bf16[128,512]{1,0:T(8,128)(2,1)S(1)} %get-tuple-element.42), channel_id=1, source_target_pairs={{0,4},{1,5},{2,6},{3,7},{4,0},{5,1},{6,2},{7,3},{8,12},{9,13},{10,... | collective-permute-start | bytes 393224 | tf_op jit(solution)/shard_map/ppermute | solution.py:401
  17.5 0.0 collective-permute-start.11
  17.5 0.0 collective-permute-done.4.refs_2_
  17.5 0.0 collective-permute-done.5.refs_3_
  17.6 2.0 %collective-permute-start.6 = (bf16[128,128]{1,0:T(8,128)(2,1)S(1)}, bf16[128,128]{1,0:T(8,128)(2,1)S(1)}, u32[]{:S(2)}, u32[]{:S(2)}) collective-permute-start(bf16[128,128]{1,0:T(8,128)(2,1)S(1)} %get-tuple-element.38.refs_1_), channel_id=1, source_target_pairs={{0,4},{1,5},{2,6},{3,7},{4,0},{5,1},{6,2},{7,3},{8,12},{9,13},{10,... | collective-permute-start | bytes 98312 | tf_op jit(solution)/shard_map/ppermute | solution.py:401
  19.6 0.8 %collective-permute-start.7 = (bf16[128,128]{1,0:T(8,128)(2,1)S(1)}, bf16[128,128]{1,0:T(8,128)(2,1)S(1)}, u32[]{:S(2)}, u32[]{:S(2)}) collective-permute-start(bf16[128,128]{1,0:T(8,128)(2,1)S(1)} %get-tuple-element.39.refs_2_), channel_id=1, source_target_pairs={{0,1},{1,0},{2,3},{3,2},{4,8},{5,9},{6,10},{7,11},{8,4},{9,5},{10,... | collective-permute-start | bytes 98312 | tf_op jit(solution)/shard_map/ppermute | solution.py:401
  20.4 1.1 %collective-permute-done.6.refs_3_ = bf16[128,128]{1,0:T(8,128)(2,1)S(1)} collective-permute-done((bf16[128,128]{1,0:T(8,128)(2,1)S(1)}, bf16[128,128]{1,0:T(8,128)(2,1)S(1)}, u32[]{:S(2)}, u32[]{:S(2)}) %collective-permute-start.6) | collective-permute-done | bytes 32800 | tf_op jit(solution)/shard_map/ppermute | solution.py:401
  21.5 0.0 collective-permute-done.7.refs_4_
  21.5 0.0 collective-permute-done.10.refs_8_
  21.5 0.0 collective-permute-done.11.refs_9_
  21.6 4.9 %shard_map.80 = f32[256,256]{1,0:T(8,128)} custom-call(f32[256,256]{1,0:T(8,128)S(1)} %get-tuple-element.35.refs_0_, bf16[128,128]{1,0:T(8,128)(2,1)S(1)} %get-tuple-element.38.refs_1_, bf16[128,128]{1,0:T(8,128)(2,1)S(1)} %get-tuple-element.39.refs_2_, bf16[128,128]{1,0:T(8,128)(2,1)S(1)} %collective-permute-done.6.refs_3_, ...), custom_call_target="tpu_custom_call" | custom-call | flops 5500000256 | bytes 65536 | tf_op jit(solution)/shard_map/pallas_call | solution.py:414
  (3 shorter events, 0.1 us)
Async XLA Ops:
  0.0 0.9 %copy-start.1 = (f32[256,256]{1,0:T(8,128)S(1)}, f32[256,256]{1,0:T(8,128)}, u32[]{:S(2)}) copy-start(f32[256,256]{1,0:T(8,128)} %mask_ref.1) | copy-start | bytes 786436
  1.0 2.6 %copy-start.5 = (bf16[384,256]{1,0:T(8,128)(2,1)S(1)}, bf16[384,256]{1,0:T(8,128)(2,1)}, u32[]{:S(2)}) copy-start(bf16[384,256]{1,0:T(8,128)(2,1)} %constant.7.clone.table_ref) | copy-start | bytes 589828
  1.1 4.1 %collective-permute-start = (bf16[128,128]{1,0:T(8,128)(2,1)S(1)}, bf16[128,128]{1,0:T(8,128)(2,1)S(1)}, u32[]{:S(2)}, u32[]{:S(2)}) collective-permute-start(bf16[128,128]{1,0:T(8,128)(2,1)S(1)} %get-tuple-element.27.after_ref), channel_id=1, source_target_pairs={{0,1},{1,2},{2,3},{3,0},{4,5},{5,6},{6,7},{7,4},{8,9},{9,10},{10,1... | collective-permute-start | bytes 98312 | tf_op jit(solution)/shard_map/ppermute | solution.py:401
  1.6 2.0 %copy-start.3 = (f32[12]{0:T(128)S(1)}, f32[12]{0:T(128)}, u32[]{:S(2)}) copy-start(f32[12]{0:T(128)} %param.10) | copy-start | bytes 148
  1.6 3.7 %collective-permute-start.1 = (bf16[128,128]{1,0:T(8,128)(2,1)S(1)}, bf16[128,128]{1,0:T(8,128)(2,1)S(1)}, u32[]{:S(2)}, u32[]{:S(2)}) collective-permute-start(bf16[128,128]{1,0:T(8,128)(2,1)S(1)} %get-tuple-element.28), channel_id=1, source_target_pairs={{0,3},{1,0},{2,1},{3,2},{4,7},{5,4},{6,5},{7,6},{8,11},{9,8},{10,9... | collective-permute-start | bytes 98312 | tf_op jit(solution)/shard_map/ppermute | solution.py:401
  5.3 3.9 %copy-start.2 = (bf16[256,256]{1,0:T(8,128)(2,1)S(1)}, bf16[256,256]{1,0:T(8,128)(2,1)}, u32[]{:S(2)}) copy-start(bf16[256,256]{1,0:T(8,128)(2,1)} %target_ref.1) | copy-start | bytes 393220
  5.5 5.5 %collective-permute-start.2 = (bf16[64,128]{1,0:T(8,128)(2,1)S(1)}, bf16[64,128]{1,0:T(8,128)(2,1)S(1)}, u32[]{:S(2)}, u32[]{:S(2)}) collective-permute-start(bf16[64,128]{1,0:T(8,128)(2,1)S(1)} %get-tuple-element.31.after_ref), channel_id=1, source_target_pairs={{0,4},{1,5},{2,6},{3,7},{4,0},{5,1},{6,2},{7,3},{8,12},{9,13},{10,... | collective-permute-start | bytes 49160 | tf_op jit(solution)/shard_map/ppermute | solution.py:401
  7.8 3.2 %copy-start = (f32[12,64,128]{2,1,0:T(8,128)S(1)}, f32[12,64,128]{2,1,0:T(8,128)}, u32[]{:S(2)}) copy-start(f32[12,64,128]{2,1,0:T(8,128)} %refs_10_.1) | copy-start | bytes 1179652
  7.8 3.2 %copy-start.4 = (bf16[1984,256]{1,0:T(8,128)(2,1)S(1)}, bf16[1984,256]{1,0:T(8,128)(2,1)}, u32[]{:S(2)}) copy-start(bf16[1984,256]{1,0:T(8,128)(2,1)} %constant.6.clone.refs_8_.refs_16_) | copy-start | bytes 3047428
  7.8 3.2 %copy-start.6 = (f32[264,128]{1,0:T(8,128)S(1)}, f32[264,128]{1,0:T(8,128)}, u32[]{:S(2)}) copy-start(f32[264,128]{1,0:T(8,128)} %constant.8.clone.refs_9_.refs_17_) | copy-start | bytes 405508
  7.8 3.2 %collective-permute-start.3 = (bf16[64,128]{1,0:T(8,128)(2,1)S(1)}, bf16[64,128]{1,0:T(8,128)(2,1)S(1)}, u32[]{:S(2)}, u32[]{:S(2)}) collective-permute-start(bf16[64,128]{1,0:T(8,128)(2,1)S(1)} %get-tuple-element.32), channel_id=1, source_target_pairs={{0,1},{1,0},{2,3},{3,2},{4,8},{5,9},{6,10},{7,11},{8,4},{9,5},{10,... | collective-permute-start | bytes 49160 | tf_op jit(solution)/shard_map/ppermute | solution.py:401
  9.2 6.4 %collective-permute-start.8 = (bf16[256,128]{1,0:T(8,128)(2,1)S(1)}, bf16[256,128]{1,0:T(8,128)(2,1)S(1)}, u32[]{:S(2)}, u32[]{:S(2)}) collective-permute-start(bf16[256,128]{1,0:T(8,128)(2,1)S(1)} %get-tuple-element.40), channel_id=1, source_target_pairs={{0,1},{1,2},{2,3},{3,0},{4,5},{5,6},{6,7},{7,4},{8,9},{9,10},{10,1... | collective-permute-start | bytes 196616 | tf_op jit(solution)/shard_map/ppermute | solution.py:401
  9.3 6.3 %collective-permute-start.9 = (bf16[256,128]{1,0:T(8,128)(2,1)S(1)}, bf16[256,128]{1,0:T(8,128)(2,1)S(1)}, u32[]{:S(2)}, u32[]{:S(2)}) collective-permute-start(bf16[256,128]{1,0:T(8,128)(2,1)S(1)} %get-tuple-element.41), channel_id=1, source_target_pairs={{0,3},{1,0},{2,1},{3,2},{4,7},{5,4},{6,5},{7,6},{8,11},{9,8},{10,9... | collective-permute-start | bytes 196616 | tf_op jit(solution)/shard_map/ppermute | solution.py:401
  13.8 3.8 %collective-permute-start.4 = (bf16[128,128]{1,0:T(8,128)(2,1)S(1)}, bf16[128,128]{1,0:T(8,128)(2,1)S(1)}, u32[]{:S(2)}, u32[]{:S(2)}) collective-permute-start(bf16[128,128]{1,0:T(8,128)(2,1)S(1)} %get-tuple-element.37.refs_1_), channel_id=1, source_target_pairs={{0,1},{1,2},{2,3},{3,0},{4,5},{5,6},{6,7},{7,4},{8,9},{9,10},{10,1... | collective-permute-start | bytes 98312 | tf_op jit(solution)/shard_map/ppermute | solution.py:401
  13.8 3.7 %collective-permute-start.5 = (bf16[128,128]{1,0:T(8,128)(2,1)S(1)}, bf16[128,128]{1,0:T(8,128)(2,1)S(1)}, u32[]{:S(2)}, u32[]{:S(2)}) collective-permute-start(bf16[128,128]{1,0:T(8,128)(2,1)S(1)} %get-tuple-element.36.refs_0_), channel_id=1, source_target_pairs={{0,3},{1,0},{2,1},{3,2},{4,7},{5,4},{6,5},{7,6},{8,11},{9,8},{10,9... | collective-permute-start | bytes 98312 | tf_op jit(solution)/shard_map/ppermute | solution.py:401
  15.6 5.9 %collective-permute-start.10 = (bf16[128,512]{1,0:T(8,128)(2,1)S(1)}, bf16[128,512]{1,0:T(8,128)(2,1)S(1)}, u32[]{:S(2)}, u32[]{:S(2)}) collective-permute-start(bf16[128,512]{1,0:T(8,128)(2,1)S(1)} %get-tuple-element.42), channel_id=1, source_target_pairs={{0,4},{1,5},{2,6},{3,7},{4,0},{5,1},{6,2},{7,3},{8,12},{9,13},{10,... | collective-permute-start | bytes 393224 | tf_op jit(solution)/shard_map/ppermute | solution.py:401
  17.5 4.0 %collective-permute-start.11 = (bf16[128,512]{1,0:T(8,128)(2,1)S(1)}, bf16[128,512]{1,0:T(8,128)(2,1)S(1)}, u32[]{:S(2)}, u32[]{:S(2)}) collective-permute-start(bf16[128,512]{1,0:T(8,128)(2,1)S(1)} %get-tuple-element.43), channel_id=1, source_target_pairs={{0,1},{1,0},{2,3},{3,2},{4,8},{5,9},{6,10},{7,11},{8,4},{9,5},{10,... | collective-permute-start | bytes 393224 | tf_op jit(solution)/shard_map/ppermute | solution.py:401
  17.6 4.0 %collective-permute-start.6 = (bf16[128,128]{1,0:T(8,128)(2,1)S(1)}, bf16[128,128]{1,0:T(8,128)(2,1)S(1)}, u32[]{:S(2)}, u32[]{:S(2)}) collective-permute-start(bf16[128,128]{1,0:T(8,128)(2,1)S(1)} %get-tuple-element.38.refs_1_), channel_id=1, source_target_pairs={{0,4},{1,5},{2,6},{3,7},{4,0},{5,1},{6,2},{7,3},{8,12},{9,13},{10,... | collective-permute-start | bytes 98312 | tf_op jit(solution)/shard_map/ppermute | solution.py:401
  19.6 2.0 %collective-permute-start.7 = (bf16[128,128]{1,0:T(8,128)(2,1)S(1)}, bf16[128,128]{1,0:T(8,128)(2,1)S(1)}, u32[]{:S(2)}, u32[]{:S(2)}) collective-permute-start(bf16[128,128]{1,0:T(8,128)(2,1)S(1)} %get-tuple-element.39.refs_2_), channel_id=1, source_target_pairs={{0,1},{1,0},{2,3},{3,2},{4,8},{5,9},{6,10},{7,11},{8,4},{9,5},{10,... | collective-permute-start | bytes 98312 | tf_op jit(solution)/shard_map/ppermute | solution.py:401
where the time goes:
time: 26.6 us; the launch traced here: 26.4 us
  starting transfers between devices  14.5 us (55%)
  Pallas kernels  8.14 us (31%)
  waiting for transfers between devices  2.75 us (10%)
  local copies, waits for them, and re-layouts  0.97 us (4%)
    ppermute x12, starting transfers between devices, permuted(): return lax.ppermute(value, ('row', 'col'), pairs)  14.5 us
    pallas_call x8, Pallas kernels, call(): pl.pallas_call(kernel, out_shape=outs, in_specs=[other.get(i, VMEM_SPEC)...  8.14 us
    ppermute x12, waiting for transfers between devices, permuted(): return lax.ppermute(value, ('row', 'col'), pairs)  2.75 us
    unnamed x14, local copies, waits for them, and re-layouts  0.97 us
  transfers between devices with their start and end apart: 12, of which 3 were waited for; matrix products, arithmetic and copies ran while one was open for 0% of the time, Pallas kernels for 11%

commit v1 on v0

--- a/solution.py
+++ b/solution.py
@@ -142,20 +142,17 @@
         partials.append(partial)
     levels = []
     for w, partial in enumerate(partials):
-        chains = [jnp.zeros((COARSE, COARSE), F32)] * 2
+        level = jnp.zeros((COARSE, COARSE), F32)
         for k, part in enumerate(partial):
             real, imag = part[:, :COARSE], part[:, COARSE:]
             rotated = jnp.concatenate([part, jnp.concatenate([-imag, real], 1)], 0)
             field = dot(t.left("q_low"), rotated)
             field_ref[w * KERN + k] = field
             a_real, a_imag = field[:, :COARSE], field[:, COARSE:]
-            chains[k % 2] = chains[k % 2] + weight_ref[k : k + 1, :] * (
-                a_real * a_real + a_imag * a_imag
-            )
-        level = chains[0] + chains[1]
+            level = level + weight_ref[k : k + 1, :] * (a_real * a_real + a_imag * a_imag)
         levels.append((2.0 * level - 2.0 * threshold).astype(BF16))
-    halves = [dot(t["interp"], jnp.concatenate([level, level], 0)).astype(BF16) for level in levels]
-    cores = [dot(jnp.concatenate([half, half], 1), t["interp_t"]) for half in halves]
+    halves = [dot(t.left("interp"), level).astype(BF16) for level in levels]
+    cores = [dot(half, t["interp_t"][:COARSE]) for half in halves]
     lows = []
     for core, (_, goal, inner) in zip(cores, windows):
         rise = jnp.tanh(core)

time: 26.6 us -> 26.6 us (level)
  no operation moved by 1% of the time
where the time goes in v1:
time: 26.6 us; the launch traced here: 26.4 us
  starting transfers between devices  14.5 us (55%)
  Pallas kernels  8.15 us (31%)
  waiting for transfers between devices  2.76 us (10%)
  local copies, waits for them, and re-layouts  0.97 us (4%)
    ppermute x12, starting transfers between devices, permuted(): return lax.ppermute(value, ('row', 'col'), pairs)  14.5 us
    pallas_call x8, Pallas kernels, call(): pl.pallas_call(kernel, out_shape=outs, in_specs=[other.get(i, VMEM_SPEC)...  8.15 us
    ppermute x12, waiting for transfers between devices, permuted(): return lax.ppermute(value, ('row', 'col'), pairs)  2.76 us
    unnamed x14, local copies, waits for them, and re-layouts  0.97 us
  transfers between devices with their start and end apart: 12, of which 3 were waited for; matrix products, arithmetic and copies ran while one was open for 0% of the time, Pallas kernels for 11%

profile of v1, /device:TPU:0, one launch (start us, length us, event | category | flops | bytes accessed | tf_op | source)
XLA Modules:
  0.0 26.4 jit_solution(6554004099998777026)
XLA Ops:
  0.0 0.0 copy-start.1
  0.0 0.9 %copy-done.1 = f32[256,256]{1,0:T(8,128)S(1)} copy-done((f32[256,256]{1,0:T(8,128)S(1)}, f32[256,256]{1,0:T(8,128)}, u32[]{:S(2)}) %copy-start.1) | copy-done | bytes 262168
  1.0 0.0 copy-start.5
  1.0 0.1 shard_map.73
  1.1 0.5 %collective-permute-start = (bf16[128,128]{1,0:T(8,128)(2,1)S(1)}, bf16[128,128]{1,0:T(8,128)(2,1)S(1)}, u32[]{:S(2)}, u32[]{:S(2)}) collective-permute-start(bf16[128,128]{1,0:T(8,128)(2,1)S(1)} %get-tuple-element.27.after_ref), channel_id=1, source_target_pairs={{0,1},{1,2},{2,3},{3,0},{4,5},{5,6},{6,7},{7,4},{8,9},{9,10},{10,1... | collective-permute-start | bytes 98312 | tf_op jit(solution)/shard_map/ppermute | solution.py:398
  1.6 0.0 copy-start.3
  1.6 2.0 %collective-permute-start.1 = (bf16[128,128]{1,0:T(8,128)(2,1)S(1)}, bf16[128,128]{1,0:T(8,128)(2,1)S(1)}, u32[]{:S(2)}, u32[]{:S(2)}) collective-permute-start(bf16[128,128]{1,0:T(8,128)(2,1)S(1)} %get-tuple-element.28), channel_id=1, source_target_pairs={{0,3},{1,0},{2,1},{3,2},{4,7},{5,4},{6,5},{7,6},{8,11},{9,8},{10,9... | collective-permute-start | bytes 98312 | tf_op jit(solution)/shard_map/ppermute | solution.py:398
  3.6 0.0 copy-done.5
  3.6 0.0 copy-done.3
  3.6 0.1 shard_map.74
  3.7 1.4 %collective-permute-done.refs_1_ = bf16[128,128]{1,0:T(8,128)(2,1)S(1)} collective-permute-done((bf16[128,128]{1,0:T(8,128)(2,1)S(1)}, bf16[128,128]{1,0:T(8,128)(2,1)S(1)}, u32[]{:S(2)}, u32[]{:S(2)}) %collective-permute-start) | collective-permute-done | bytes 32800 | tf_op jit(solution)/shard_map/ppermute | solution.py:398
  5.1 0.2 collective-permute-done.1.refs_2_
  5.3 0.0 copy-start.2
  5.3 0.2 shard_map.75
  5.5 2.3 %collective-permute-start.2 = (bf16[64,128]{1,0:T(8,128)(2,1)S(1)}, bf16[64,128]{1,0:T(8,128)(2,1)S(1)}, u32[]{:S(2)}, u32[]{:S(2)}) collective-permute-start(bf16[64,128]{1,0:T(8,128)(2,1)S(1)} %get-tuple-element.31.after_ref), channel_id=1, source_target_pairs={{0,4},{1,5},{2,6},{3,7},{4,0},{5,1},{6,2},{7,3},{8,12},{9,13},{10,... | collective-permute-start | bytes 49160 | tf_op jit(solution)/shard_map/ppermute | solution.py:398
  7.8 0.0 copy-start
  7.8 0.0 copy-start.4
  7.8 0.0 copy-start.6
  7.8 1.3 %collective-permute-start.3 = (bf16[64,128]{1,0:T(8,128)(2,1)S(1)}, bf16[64,128]{1,0:T(8,128)(2,1)S(1)}, u32[]{:S(2)}, u32[]{:S(2)}) collective-permute-start(bf16[64,128]{1,0:T(8,128)(2,1)S(1)} %get-tuple-element.32), channel_id=1, source_target_pairs={{0,1},{1,0},{2,3},{3,2},{4,8},{5,9},{6,10},{7,11},{8,4},{9,5},{10,... | collective-permute-start | bytes 49160 | tf_op jit(solution)/shard_map/ppermute | solution.py:398
  9.2 0.0 copy-done.2
  9.2 0.1 collective-permute-start.8
  9.3 1.7 %collective-permute-start.9 = (bf16[256,128]{1,0:T(8,128)(2,1)S(1)}, bf16[256,128]{1,0:T(8,128)(2,1)S(1)}, u32[]{:S(2)}, u32[]{:S(2)}) collective-permute-start(bf16[256,128]{1,0:T(8,128)(2,1)S(1)} %get-tuple-element.41), channel_id=1, source_target_pairs={{0,3},{1,0},{2,1},{3,2},{4,7},{5,4},{6,5},{7,6},{8,11},{9,8},{10,9... | collective-permute-start | bytes 196616 | tf_op jit(solution)/shard_map/ppermute | solution.py:398
  11.0 0.0 collective-permute-done.2.refs_2_
  11.0 0.0 collective-permute-done.3.refs_3_
  11.0 0.0 copy-done
  11.0 0.0 copy-done.4
  11.0 0.0 copy-done.6
  11.0 2.7 %shard_map.77 = (f32[256,256]{1,0:T(8,128)S(1)}, bf16[128,128]{1,0:T(8,128)(2,1)S(1)}, bf16[128,128]{1,0:T(8,128)(2,1)S(1)}, f32[12,64,128]{2,1,0:T(8,128)S(1)},...) custom-call(f32[256,256]{1,0:T(8,128)S(1)} %get-tuple-element.26.refs_0_, ...), custom_call_target="tpu_custom_call" | custom-call | flops 3300000000 | bytes 65536 | tf_op jit(solution)/shard_map/pallas_call | solution.py:411
  13.7 0.1 collective-permute-start.4
  13.8 1.7 %collective-permute-start.5 = (bf16[128,128]{1,0:T(8,128)(2,1)S(1)}, bf16[128,128]{1,0:T(8,128)(2,1)S(1)}, u32[]{:S(2)}, u32[]{:S(2)}) collective-permute-start(bf16[128,128]{1,0:T(8,128)(2,1)S(1)} %get-tuple-element.36.refs_0_), channel_id=1, source_target_pairs={{0,3},{1,0},{2,1},{3,2},{4,7},{5,4},{6,5},{7,6},{8,11},{9,8},{10,9... | collective-permute-start | bytes 98312 | tf_op jit(solution)/shard_map/ppermute | solution.py:398
  15.5 0.0 collective-permute-done.8.left_ref.refs_6_
  15.5 0.0 collective-permute-done.9.right_ref.refs_7_
  15.6 1.9 %collective-permute-start.10 = (bf16[128,512]{1,0:T(8,128)(2,1)S(1)}, bf16[128,512]{1,0:T(8,128)(2,1)S(1)}, u32[]{:S(2)}, u32[]{:S(2)}) collective-permute-start(bf16[128,512]{1,0:T(8,128)(2,1)S(1)} %get-tuple-element.42), channel_id=1, source_target_pairs={{0,4},{1,5},{2,6},{3,7},{4,0},{5,1},{6,2},{7,3},{8,12},{9,13},{10,... | collective-permute-start | bytes 393224 | tf_op jit(solution)/shard_map/ppermute | solution.py:398
  17.5 0.0 collective-permute-start.11
  17.5 0.0 collective-permute-done.4.refs_2_
  17.5 0.0 collective-permute-done.5.refs_3_
  17.5 2.0 %collective-permute-start.6 = (bf16[128,128]{1,0:T(8,128)(2,1)S(1)}, bf16[128,128]{1,0:T(8,128)(2,1)S(1)}, u32[]{:S(2)}, u32[]{:S(2)}) collective-permute-start(bf16[128,128]{1,0:T(8,128)(2,1)S(1)} %get-tuple-element.38.refs_1_), channel_id=1, source_target_pairs={{0,4},{1,5},{2,6},{3,7},{4,0},{5,1},{6,2},{7,3},{8,12},{9,13},{10,... | collective-permute-start | bytes 98312 | tf_op jit(solution)/shard_map/ppermute | solution.py:398
  19.6 0.8 %collective-permute-start.7 = (bf16[128,128]{1,0:T(8,128)(2,1)S(1)}, bf16[128,128]{1,0:T(8,128)(2,1)S(1)}, u32[]{:S(2)}, u32[]{:S(2)}) collective-permute-start(bf16[128,128]{1,0:T(8,128)(2,1)S(1)} %get-tuple-element.39.refs_2_), channel_id=1, source_target_pairs={{0,1},{1,0},{2,3},{3,2},{4,8},{5,9},{6,10},{7,11},{8,4},{9,5},{10,... | collective-permute-start | bytes 98312 | tf_op jit(solution)/shard_map/ppermute | solution.py:398
  20.4 1.1 %collective-permute-done.6.refs_3_ = bf16[128,128]{1,0:T(8,128)(2,1)S(1)} collective-permute-done((bf16[128,128]{1,0:T(8,128)(2,1)S(1)}, bf16[128,128]{1,0:T(8,128)(2,1)S(1)}, u32[]{:S(2)}, u32[]{:S(2)}) %collective-permute-start.6) | collective-permute-done | bytes 32800 | tf_op jit(solution)/shard_map/ppermute | solution.py:398
  21.5 0.0 collective-permute-done.7.refs_4_
  21.5 0.0 collective-permute-done.10.refs_8_
  21.5 0.0 collective-permute-done.11.refs_9_
  21.5 4.9 %shard_map.80 = f32[256,256]{1,0:T(8,128)} custom-call(f32[256,256]{1,0:T(8,128)S(1)} %get-tuple-element.35.refs_0_, bf16[128,128]{1,0:T(8,128)(2,1)S(1)} %get-tuple-element.38.refs_1_, bf16[128,128]{1,0:T(8,128)(2,1)S(1)} %get-tuple-element.39.refs_2_, bf16[128,128]{1,0:T(8,128)(2,1)S(1)} %collective-permute-done.6.refs_3_, ...), custom_call_target="tpu_custom_call" | custom-call | flops 5500000256 | bytes 65536 | tf_op jit(solution)/shard_map/pallas_call | solution.py:411
  (3 shorter events, 0.1 us)
Async XLA Ops:
  0.0 0.9 %copy-start.1 = (f32[256,256]{1,0:T(8,128)S(1)}, f32[256,256]{1,0:T(8,128)}, u32[]{:S(2)}) copy-start(f32[256,256]{1,0:T(8,128)} %mask_ref.1) | copy-start | bytes 786436
  1.0 2.6 %copy-start.5 = (bf16[384,256]{1,0:T(8,128)(2,1)S(1)}, bf16[384,256]{1,0:T(8,128)(2,1)}, u32[]{:S(2)}) copy-start(bf16[384,256]{1,0:T(8,128)(2,1)} %constant.7.clone.table_ref) | copy-start | bytes 589828
  1.1 4.1 %collective-permute-start = (bf16[128,128]{1,0:T(8,128)(2,1)S(1)}, bf16[128,128]{1,0:T(8,128)(2,1)S(1)}, u32[]{:S(2)}, u32[]{:S(2)}) collective-permute-start(bf16[128,128]{1,0:T(8,128)(2,1)S(1)} %get-tuple-element.27.after_ref), channel_id=1, source_target_pairs={{0,1},{1,2},{2,3},{3,0},{4,5},{5,6},{6,7},{7,4},{8,9},{9,10},{10,1... | collective-permute-start | bytes 98312 | tf_op jit(solution)/shard_map/ppermute | solution.py:398
  1.6 2.0 %copy-start.3 = (f32[12]{0:T(128)S(1)}, f32[12]{0:T(128)}, u32[]{:S(2)}) copy-start(f32[12]{0:T(128)} %param.10) | copy-start | bytes 148
  1.6 3.7 %collective-permute-start.1 = (bf16[128,128]{1,0:T(8,128)(2,1)S(1)}, bf16[128,128]{1,0:T(8,128)(2,1)S(1)}, u32[]{:S(2)}, u32[]{:S(2)}) collective-permute-start(bf16[128,128]{1,0:T(8,128)(2,1)S(1)} %get-tuple-element.28), channel_id=1, source_target_pairs={{0,3},{1,0},{2,1},{3,2},{4,7},{5,4},{6,5},{7,6},{8,11},{9,8},{10,9... | collective-permute-start | bytes 98312 | tf_op jit(solution)/shard_map/ppermute | solution.py:398
  5.3 3.9 %copy-start.2 = (bf16[256,256]{1,0:T(8,128)(2,1)S(1)}, bf16[256,256]{1,0:T(8,128)(2,1)}, u32[]{:S(2)}) copy-start(bf16[256,256]{1,0:T(8,128)(2,1)} %target_ref.1) | copy-start | bytes 393220
  5.5 5.5 %collective-permute-start.2 = (bf16[64,128]{1,0:T(8,128)(2,1)S(1)}, bf16[64,128]{1,0:T(8,128)(2,1)S(1)}, u32[]{:S(2)}, u32[]{:S(2)}) collective-permute-start(bf16[64,128]{1,0:T(8,128)(2,1)S(1)} %get-tuple-element.31.after_ref), channel_id=1, source_target_pairs={{0,4},{1,5},{2,6},{3,7},{4,0},{5,1},{6,2},{7,3},{8,12},{9,13},{10,... | collective-permute-start | bytes 49160 | tf_op jit(solution)/shard_map/ppermute | solution.py:398
  7.8 3.2 %copy-start = (f32[12,64,128]{2,1,0:T(8,128)S(1)}, f32[12,64,128]{2,1,0:T(8,128)}, u32[]{:S(2)}) copy-start(f32[12,64,128]{2,1,0:T(8,128)} %refs_10_.1) | copy-start | bytes 1179652
  7.8 3.2 %copy-start.4 = (bf16[1984,256]{1,0:T(8,128)(2,1)S(1)}, bf16[1984,256]{1,0:T(8,128)(2,1)}, u32[]{:S(2)}) copy-start(bf16[1984,256]{1,0:T(8,128)(2,1)} %constant.6.clone.refs_8_.refs_16_) | copy-start | bytes 3047428
  7.8 3.2 %copy-start.6 = (f32[264,128]{1,0:T(8,128)S(1)}, f32[264,128]{1,0:T(8,128)}, u32[]{:S(2)}) copy-start(f32[264,128]{1,0:T(8,128)} %constant.8.clone.refs_9_.refs_17_) | copy-start | bytes 405508
  7.8 3.2 %collective-permute-start.3 = (bf16[64,128]{1,0:T(8,128)(2,1)S(1)}, bf16[64,128]{1,0:T(8,128)(2,1)S(1)}, u32[]{:S(2)}, u32[]{:S(2)}) collective-permute-start(bf16[64,128]{1,0:T(8,128)(2,1)S(1)} %get-tuple-element.32), channel_id=1, source_target_pairs={{0,1},{1,0},{2,3},{3,2},{4,8},{5,9},{6,10},{7,11},{8,4},{9,5},{10,... | collective-permute-start | bytes 49160 | tf_op jit(solution)/shard_map/ppermute | solution.py:398
  9.2 6.3 %collective-permute-start.8 = (bf16[256,128]{1,0:T(8,128)(2,1)S(1)}, bf16[256,128]{1,0:T(8,128)(2,1)S(1)}, u32[]{:S(2)}, u32[]{:S(2)}) collective-permute-start(bf16[256,128]{1,0:T(8,128)(2,1)S(1)} %get-tuple-element.40), channel_id=1, source_target_pairs={{0,1},{1,2},{2,3},{3,0},{4,5},{5,6},{6,7},{7,4},{8,9},{9,10},{10,1... | collective-permute-start | bytes 196616 | tf_op jit(solution)/shard_map/ppermute | solution.py:398
  9.3 6.3 %collective-permute-start.9 = (bf16[256,128]{1,0:T(8,128)(2,1)S(1)}, bf16[256,128]{1,0:T(8,128)(2,1)S(1)}, u32[]{:S(2)}, u32[]{:S(2)}) collective-permute-start(bf16[256,128]{1,0:T(8,128)(2,1)S(1)} %get-tuple-element.41), channel_id=1, source_target_pairs={{0,3},{1,0},{2,1},{3,2},{4,7},{5,4},{6,5},{7,6},{8,11},{9,8},{10,9... | collective-permute-start | bytes 196616 | tf_op jit(solution)/shard_map/ppermute | solution.py:398
  13.7 3.8 %collective-permute-start.4 = (bf16[128,128]{1,0:T(8,128)(2,1)S(1)}, bf16[128,128]{1,0:T(8,128)(2,1)S(1)}, u32[]{:S(2)}, u32[]{:S(2)}) collective-permute-start(bf16[128,128]{1,0:T(8,128)(2,1)S(1)} %get-tuple-element.37.refs_1_), channel_id=1, source_target_pairs={{0,1},{1,2},{2,3},{3,0},{4,5},{5,6},{6,7},{7,4},{8,9},{9,10},{10,1... | collective-permute-start | bytes 98312 | tf_op jit(solution)/shard_map/ppermute | solution.py:398
  13.8 3.7 %collective-permute-start.5 = (bf16[128,128]{1,0:T(8,128)(2,1)S(1)}, bf16[128,128]{1,0:T(8,128)(2,1)S(1)}, u32[]{:S(2)}, u32[]{:S(2)}) collective-permute-start(bf16[128,128]{1,0:T(8,128)(2,1)S(1)} %get-tuple-element.36.refs_0_), channel_id=1, source_target_pairs={{0,3},{1,0},{2,1},{3,2},{4,7},{5,4},{6,5},{7,6},{8,11},{9,8},{10,9... | collective-permute-start | bytes 98312 | tf_op jit(solution)/shard_map/ppermute | solution.py:398
  15.6 5.9 %collective-permute-start.10 = (bf16[128,512]{1,0:T(8,128)(2,1)S(1)}, bf16[128,512]{1,0:T(8,128)(2,1)S(1)}, u32[]{:S(2)}, u32[]{:S(2)}) collective-permute-start(bf16[128,512]{1,0:T(8,128)(2,1)S(1)} %get-tuple-element.42), channel_id=1, source_target_pairs={{0,4},{1,5},{2,6},{3,7},{4,0},{5,1},{6,2},{7,3},{8,12},{9,13},{10,... | collective-permute-start | bytes 393224 | tf_op jit(solution)/shard_map/ppermute | solution.py:398
  17.5 4.0 %collective-permute-start.11 = (bf16[128,512]{1,0:T(8,128)(2,1)S(1)}, bf16[128,512]{1,0:T(8,128)(2,1)S(1)}, u32[]{:S(2)}, u32[]{:S(2)}) collective-permute-start(bf16[128,512]{1,0:T(8,128)(2,1)S(1)} %get-tuple-element.43), channel_id=1, source_target_pairs={{0,1},{1,0},{2,3},{3,2},{4,8},{5,9},{6,10},{7,11},{8,4},{9,5},{10,... | collective-permute-start | bytes 393224 | tf_op jit(solution)/shard_map/ppermute | solution.py:398
  17.5 4.0 %collective-permute-start.6 = (bf16[128,128]{1,0:T(8,128)(2,1)S(1)}, bf16[128,128]{1,0:T(8,128)(2,1)S(1)}, u32[]{:S(2)}, u32[]{:S(2)}) collective-permute-start(bf16[128,128]{1,0:T(8,128)(2,1)S(1)} %get-tuple-element.38.refs_1_), channel_id=1, source_target_pairs={{0,4},{1,5},{2,6},{3,7},{4,0},{5,1},{6,2},{7,3},{8,12},{9,13},{10,... | collective-permute-start | bytes 98312 | tf_op jit(solution)/shard_map/ppermute | solution.py:398
  19.6 2.0 %collective-permute-start.7 = (bf16[128,128]{1,0:T(8,128)(2,1)S(1)}, bf16[128,128]{1,0:T(8,128)(2,1)S(1)}, u32[]{:S(2)}, u32[]{:S(2)}) collective-permute-start(bf16[128,128]{1,0:T(8,128)(2,1)S(1)} %get-tuple-element.39.refs_2_), channel_id=1, source_target_pairs={{0,1},{1,0},{2,3},{3,2},{4,8},{5,9},{6,10},{7,11},{8,4},{9,5},{10,... | collective-permute-start | bytes 98312 | tf_op jit(solution)/shard_map/ppermute | solution.py:398
